TPU v7x, 32 devices: a whole 2x2x4 slice. The times are simulated.
32 devices in a mesh: gx: 4 (over z), gy: 8 (over y, x, core).
Axes of the slice: x: 2, y: 2, z: 4, core: 2. Of those that a mesh axis runs over, the one named last changes fastest.
Arguments:
- die_basis: float32 [64, 256, 512], P('gx', 'gy'), may hold values from -0.078125 to 0.078125
- die_coeff: float32 [5, 64, 256], P(None, 'gx', 'gy'), may hold values from 0.2 to 5
- pkg_basis: float32 [1024, 64, 512], P(('gx', 'gy')), may hold values from -0.09375 to 0.09375
- send_blocks: int32 [32, 4, 4], P(('gx', 'gy')), may hold values from 0 to 31
- columns: int32 [5, 1024, 4], P(None, ('gx', 'gy')), may hold values from 0 to 47
- counts: int32 [5, 1024], P(None, ('gx', 'gy')), may hold values from 1 to 4
- pkg_blocks: float32 [5, 1024, 64, 256], P(None, ('gx', 'gy')), may hold values from -48 to 48
Outputs:
- reduced: float32 [5, 512, 512], replicated
Inputs may be any that keep to these rules, and one draw needn't show every extreme that they name: `columns`: indices below 32 name the partition's own blocks, the others its ghost blocks in the order of the statement.
All inputs are finite; a program needn't handle non-finite values.
Results may differ from a plain program's by a relative error of at most 0.0001.
Values sent between devices are 32-bit elements; how exact they have to be, the bound alone decides.
No kernel may reach another device: no remote copies, remote signals or barrier semaphores. Data moves between devices by JAX's collectives and lax.ppermute only.
A program may use at most 256 MiB of HBM per device.

v0:
```python
import jax
import jax.numpy as jnp
from jax import lax
from jax.sharding import PartitionSpec as P

highest = lax.Precision.HIGHEST


def from_behind(value, axis, steps):
    count = lax.axis_size(axis)
    leading, last = (max(0, -steps), min(count, count - steps))
    return lax.ppermute(value, axis, [(source, source + steps) for source in range(leading, last)])


def passed_along(value, axis, steps):
    count = lax.axis_size(axis)
    pairs = [(source, (source + steps) % count) for source in range(count)]
    return lax.ppermute(value, axis, pairs)


def weighted_gram(weights, field):
    width = field.shape[-1]
    flat = field.reshape(-1, width)
    scaled = weights.reshape(-1, 1) * flat
    return lax.dot_general(
        flat,
        scaled,
        (((0,), (0,)), ((), ())),
        precision=highest,
        preferred_element_type=jnp.float32,
    )


def die_terms(basis, coeff, next_x_row, next_y_col):
    next_x = jnp.concatenate([basis[1:], next_x_row], axis=0)
    next_y = jnp.concatenate([basis[:, 1:], next_y_col], axis=1)
    diff_x = basis - next_x
    diff_y = basis - next_y
    return jnp.stack(
        [
            weighted_gram(coeff[0], basis),
            weighted_gram(coeff[1], diff_x),
            weighted_gram(coeff[2], diff_y),
            weighted_gram(coeff[3], basis),
            weighted_gram(coeff[4], diff_x) + weighted_gram(coeff[4], diff_y),
        ]
    )


def package_terms(owned, table, columns, counts, blocks):
    row_count = owned.shape[0]
    block = owned.shape[1]
    width = owned.shape[2]
    entries = columns.shape[-1]
    results = []
    for term_idx in range(columns.shape[0]):
        picked = table[columns[term_idx]]
        live = (jnp.arange(entries, dtype=jnp.int32)[None, :] < counts[term_idx][:, None]).astype(
            jnp.float32
        )
        matrices = (
            blocks[term_idx].reshape(row_count, block, entries, block) * live[:, None, :, None]
        )
        image = jnp.einsum("rinj,rnjk->rik", matrices, picked, precision=highest)
        results.append(
            lax.dot_general(
                owned.reshape(-1, width),
                image.reshape(-1, width),
                (((0,), (0,)), ((), ())),
                precision=highest,
                preferred_element_type=jnp.float32,
            )
        )
    return jnp.stack(results)


def body(die_basis, die_coeff, pkg_basis, send_blocks, columns, counts, pkg_blocks):
    next_x_row = from_behind(die_basis[:1], "gx", -1)
    next_y_col = from_behind(die_basis[:, :1], "gy", -1)
    lists = send_blocks[0]
    from_lower_x = passed_along(pkg_basis[lists[0]], "gx", 1)
    from_upper_x = passed_along(pkg_basis[lists[1]], "gx", -1)
    from_lower_y = passed_along(pkg_basis[lists[2]], "gy", 1)
    from_upper_y = passed_along(pkg_basis[lists[3]], "gy", -1)
    table = jnp.concatenate(
        [pkg_basis, from_lower_x, from_upper_x, from_lower_y, from_upper_y], axis=0
    )
    partial_terms = die_terms(die_basis, die_coeff, next_x_row, next_y_col)
    partial_terms = partial_terms + package_terms(pkg_basis, table, columns, counts, pkg_blocks)
    return lax.psum(partial_terms, ("gx", "gy"))


def solution(mesh):
    placed = (
        P("gx", "gy", None),
        P(None, "gx", "gy"),
        P(("gx", "gy"), None, None),
        P(("gx", "gy"), None, None),
        P(None, ("gx", "gy"), None),
        P(None, ("gx", "gy")),
        P(None, ("gx", "gy"), None, None),
    )
    return jax.shard_map(body, mesh=mesh, in_specs=placed, out_specs=P(), check_vma=False)
```

profile of v0, /device:TPU:0, one launch (start us, length us, event | category | flops | bytes accessed | tf_op | source)
XLA Modules:
  0.0 460.3 jit_solution(5091545625883094443)
XLA Ops:
  7.4 3.6 gather_fusion
  11.0 3.1 collective-permute-start.2
  14.0 3.6 gather_fusion.1
  17.6 2.0 collective-permute-start.3
  19.6 3.6 gather_fusion.2
  23.2 3.6 gather_fusion.3
  26.8 2.6 collective-permute-start.5
  30.8 4.9 %constant_dynamic-update-slice_fusion.4 = f32[48,64,512]{2,1,0:T(8,128)} fusion(f32[32,64,512]{2,1,0:T(8,128)} %param.9), kind=kLoop, calls=%fused_computation.81 | loop fusion | bytes 8388608
  36.1 7.9 %fusion.120 = (f32[1,32,64,256]{3,2,1,0:T(8,128)S(1)}, f32[1,32,64,256]{3,2,1,0:T(8,128)}, f32[1,32,64,256]{3,2,1,0:T(8,128)}, f32[1,32,64,256]{3,2,1,0:T(8,128)}, f32[1,32,64,256]{3,2,1,0:T(8,128)}) fusion(f32[5,32,64,256]{3,2,1,0:T(8,128)} %param.13), kind=kLoop, calls=%fused_computation.128 | loop fusion | bytes 20971520 | tf_op jit(solution)/shard_map/slice | solution.py:62
  44.0 5.1 %reshape_squeeze.22 = f32[32,64,4,64]{3,2,1,0:T(4,128)} reshape(f32[1,32,64,256]{3,2,1,0:T(8,128)} %get-tuple-element.7) | data formatting | bytes 4194304 | tf_op jit(solution)/shard_map/reshape;squeeze | solution.py:62
  49.3 5.1 %reshape_squeeze.10 = f32[32,64,4,64]{3,2,1,0:T(4,128)} reshape(f32[1,32,64,256]{3,2,1,0:T(8,128)} %get-tuple-element.8) | data formatting | bytes 4194304 | tf_op jit(solution)/shard_map/reshape;squeeze | solution.py:62
  54.3 5.1 %reshape_squeeze.23 = f32[32,64,4,64]{3,2,1,0:T(4,128)} reshape(f32[1,32,64,256]{3,2,1,0:T(8,128)} %get-tuple-element.6) | data formatting | bytes 4194304 | tf_op jit(solution)/shard_map/reshape;squeeze | solution.py:62
  59.8 5.1 %reshape_squeeze.24 = f32[32,64,4,64]{3,2,1,0:T(4,128)} reshape(f32[1,32,64,256]{3,2,1,0:T(8,128)} %get-tuple-element.9) | data formatting | bytes 4194304 | tf_op jit(solution)/shard_map/reshape;squeeze | solution.py:62
  64.9 3.5 reshape_squeeze.25
  68.5 2.0 fusion.35
  70.6 2.9 broadcast_multiply_fusion.3
  73.5 2.9 broadcast_multiply_fusion.4
  76.6 2.9 broadcast_multiply_fusion.2
  79.5 2.9 broadcast_multiply_fusion.1
  82.5 3.0 broadcast_multiply_fusion
  87.2 2.2 fusion.59
  89.4 3.0 collective-permute-done
  92.4 2.1 fusion.41
  94.5 2.2 fusion.47
  96.8 2.0 fusion.53
  98.8 2.2 fusion.98
  101.0 2.3 copy-done.10
  105.2 1.9 constant_dynamic-update-slice_fusion.2
  107.1 1.9 constant_dynamic-update-slice_fusion.1
  109.0 1.9 constant_dynamic-update-slice_fusion
  110.8 12.9 %gather_fusion.5 = f32[128,64,512]{2,1,0:T(8,128)} fusion(f32[48,64,512]{2,1,0:T(8,128)} %constant_dynamic-update-slice_fusion, s32[1024]{0:T(1024)S(1)} %get-tuple-element.32), kind=kCustom, calls=%fused_computation.5 | custom fusion | bytes 33554944 | tf_op jit(solution)/shard_map/gather | solution.py:57
  123.7 12.7 %gather_fusion.4 = f32[128,64,512]{2,1,0:T(8,128)} fusion(f32[48,64,512]{2,1,0:T(8,128)} %constant_dynamic-update-slice_fusion, s32[1024]{0:T(1024)S(1)} %pad_clamp_fusion.4), kind=kCustom, calls=%fused_computation.4 | custom fusion | bytes 33554944 | tf_op jit(solution)/shard_map/gather | solution.py:57
  136.4 13.9 %fusion.18 = f32[32,64,512,1]{2,1,3,0:T(8,128)S(1)} fusion(f32[32,4,64,512]{3,2,1,0:T(8,128)} %bitcast.211, f32[32,64,4,64]{3,2,1,0:T(4,128)} %broadcast_multiply_fusion.4), kind=kOutput, calls=%fused_computation.27 | convolution fusion | flops 3221225472 | bytes 23068672 | tf_op jit(solution)/shard_map/rinj,rnjk->rik/dot_general | solution.py:64
  150.4 8.0 %fusion.65 = f32[5,512,512]{1,2,0:T(8,128)} fusion(f32[32,64,512]{2,1,0:T(8,128)S(1)} %copy-done.9, f32[32,64,512,1]{2,1,3,0:T(8,128)S(1)} %fusion.18), kind=kOutput, calls=%fused_computation.57 | convolution fusion | flops 6442450944 | bytes 9437184 | tf_op jit(solution)/shard_map/dot_general | solution.py:66
  158.3 12.7 %gather_fusion.6 = f32[128,64,512]{2,1,0:T(8,128)} fusion(f32[48,64,512]{2,1,0:T(8,128)} %constant_dynamic-update-slice_fusion, s32[1024]{0:T(1024)S(1)} %get-tuple-element.31), kind=kCustom, calls=%fused_computation.6 | custom fusion | bytes 33554944 | tf_op jit(solution)/shard_map/gather | solution.py:57
  171.0 12.7 %gather_fusion.7 = f32[128,64,512]{2,1,0:T(8,128)} fusion(f32[48,64,512]{2,1,0:T(8,128)} %constant_dynamic-update-slice_fusion, s32[1024]{0:T(1024)S(1)} %get-tuple-element.30), kind=kCustom, calls=%fused_computation.7 | custom fusion | bytes 33554944 | tf_op jit(solution)/shard_map/gather | solution.py:57
  183.7 12.9 %gather_fusion.8 = f32[128,64,512]{2,1,0:T(8,128)} fusion(f32[48,64,512]{2,1,0:T(8,128)} %constant_dynamic-update-slice_fusion, s32[1024]{0:T(1024)S(1)} %get-tuple-element.29), kind=kCustom, calls=%fused_computation.8 | custom fusion | bytes 33554944 | tf_op jit(solution)/shard_map/gather | solution.py:57
  196.5 16.1 %fusion.16 = f32[32,64,512,1]{2,1,3,0:T(8,128)} fusion(f32[32,4,64,512]{3,2,1,0:T(8,128)} %bitcast.206, f32[32,64,4,64]{3,2,1,0:T(4,128)} %broadcast_multiply_fusion.3), kind=kOutput, calls=%fused_computation.25 | convolution fusion | flops 3221225472 | bytes 23068672 | tf_op jit(solution)/shard_map/rinj,rnjk->rik/dot_general | solution.py:64
  212.6 10.4 %fusion.71 = f32[5,512,512]{1,2,0:T(8,128)} fusion(f32[5,512,512]{1,2,0:T(8,128)} %fusion.65, f32[32,64,512]{2,1,0:T(8,128)} %param.9, f32[32,64,512,1]{2,1,3,0:T(8,128)} %fusion.16), kind=kOutput, calls=%fused_computation.59 | convolution fusion | flops 6442450944 | bytes 9437184 | tf_op jit(solution)/shard_map/dot_general | solution.py:66
  223.0 12.0 %fusion.14 = f32[32,64,512,1]{2,1,3,0:T(8,128)} fusion(f32[32,4,64,512]{3,2,1,0:T(8,128)S(1)} %bitcast.210, f32[32,64,4,64]{3,2,1,0:T(4,128)S(1)} %copy-done.6), kind=kOutput, calls=%fused_computation.23 | convolution fusion | flops 3221225472 | bytes 23068672 | tf_op jit(solution)/shard_map/rinj,rnjk->rik/dot_general | solution.py:64
  235.1 10.4 %fusion.77 = f32[5,512,512]{1,2,0:T(8,128)} fusion(f32[5,512,512]{1,2,0:T(8,128)} %fusion.71, f32[32,64,512]{2,1,0:T(8,128)} %param.9, f32[32,64,512,1]{2,1,3,0:T(8,128)} %fusion.14), kind=kOutput, calls=%fused_computation.61 | convolution fusion | flops 6442450944 | bytes 9437184 | tf_op jit(solution)/shard_map/dot_general | solution.py:66
  245.5 14.7 %fusion.12 = f32[32,64,512,1]{2,1,3,0:T(8,128)} fusion(f32[32,4,64,512]{3,2,1,0:T(8,128)} %bitcast.207, f32[32,64,4,64]{3,2,1,0:T(4,128)S(1)} %copy-done.8), kind=kOutput, calls=%fused_computation.21 | convolution fusion | flops 3221225472 | bytes 23068672 | tf_op jit(solution)/shard_map/rinj,rnjk->rik/dot_general | solution.py:64
  260.2 10.6 %fusion.83 = f32[5,512,512]{1,2,0:T(8,128)} fusion(f32[5,512,512]{1,2,0:T(8,128)} %fusion.77, f32[32,64,512]{2,1,0:T(8,128)} %param.9, f32[32,64,512,1]{2,1,3,0:T(8,128)} %fusion.12), kind=kOutput, calls=%fused_computation.63 | convolution fusion | flops 6442450944 | bytes 9437184 | tf_op jit(solution)/shard_map/dot_general | solution.py:66
  270.8 11.8 %fusion.10 = f32[32,64,512,1]{2,1,3,0:T(8,128)} fusion(f32[32,4,64,512]{3,2,1,0:T(8,128)S(1)} %bitcast.205, f32[32,64,4,64]{3,2,1,0:T(4,128)S(1)} %copy-done.7), kind=kOutput, calls=%fused_computation.19 | convolution fusion | flops 3221225472 | bytes 23068672 | tf_op jit(solution)/shard_map/rinj,rnjk->rik/dot_general | solution.py:64
  282.6 10.2 %fusion.89 = f32[5,512,512]{1,2,0:T(8,128)} fusion(f32[5,512,512]{1,2,0:T(8,128)} %fusion.83, f32[32,64,512]{2,1,0:T(8,128)} %param.9, f32[32,64,512,1]{2,1,3,0:T(8,128)} %fusion.10), kind=kOutput, calls=%fused_computation.65 | convolution fusion | flops 6442450944 | bytes 9437184 | tf_op jit(solution)/shard_map/dot_general | solution.py:66
  292.9 7.9 %add.108 = f32[5,512,512]{1,2,0:T(8,128)} add(f32[5,512,512]{1,2,0:T(8,128)} %copy-done.10, f32[5,512,512]{1,2,0:T(8,128)} %fusion.89) | non-fusion elementwise | flops 1310720 | bytes 15728640 | tf_op jit(solution)/shard_map/add | solution.py:89
  300.8 146.3 %all-reduce.2.cloned.1.call-done = f32[5,512,512]{1,2,0:T(8,128)} async-done(((f32[5,512,512]{1,2,0:T(8,128)}), f32[5,512,512]{1,2,0:T(8,128)}) %all-reduce.2.cloned.1.call-update) | async-done | bytes 5242896 | tf_op jit(solution)/shard_map/psum | solution.py:90
  447.1 5.9 %copy.27 = f32[5,512,512]{2,1,0:T(8,128)} copy(f32[5,512,512]{1,2,0:T(8,128)} %all-reduce.2.cloned.1.call-done) | data formatting | bytes 10485760 | tf_op jit(solution)/shard_map/psum | solution.py:90
  (84 shorter events, 7.1 us)
Async XLA Ops:
  6.5 22.9 %copy-start = (f32[16,32,512]{2,1,0:T(8,128)S(1)}, f32[16,32,512]{2,1,0:T(8,128)}, u32[]{:S(2)}) copy-start(f32[16,32,512]{2,1,0:T(8,128)} %param.7) | copy-start | bytes 3145732
  6.5 440.6 %all-reduce.2.cloned.1.call-start = ((), (), s32[]{:S(2)}) async-start(), calls=%async_computation | async-start | bytes 10485760 | tf_op jit(solution)/shard_map/psum | solution.py:90
  11.0 92.4 %collective-permute-start.2 = (f32[4,64,512]{2,1,0:T(8,128)}, f32[4,64,512]{2,1,0:T(8,128)}, u32[]{:S(2)}, u32[]{:S(2)}) collective-permute-start(f32[4,64,512]{2,1,0:T(8,128)} %gather_fusion), channel_id=1, source_target_pairs={{0,8},{8,16},{16,24},{24,0},{1,9},{9,17},{17,25},{25,1},{2,10},{10... | collective-permute-start | bytes 1572872 | tf_op jit(solution)/shard_map/ppermute | solution.py:18
  17.6 87.6 %collective-permute-start.3 = (f32[4,64,512]{2,1,0:T(8,128)}, f32[4,64,512]{2,1,0:T(8,128)}, u32[]{:S(2)}, u32[]{:S(2)}) collective-permute-start(f32[4,64,512]{2,1,0:T(8,128)} %gather_fusion.1), channel_id=1, source_target_pairs={{0,24},{8,0},{16,8},{24,16},{1,25},{9,1},{17,9},{25,17},{2,26},{10... | collective-permute-start | bytes 1572872 | tf_op jit(solution)/shard_map/ppermute | solution.py:18
  23.2 83.9 %collective-permute-start.4 = (f32[4,64,512]{2,1,0:T(8,128)}, f32[4,64,512]{2,1,0:T(8,128)}, u32[]{:S(2)}, u32[]{:S(2)}) collective-permute-start(f32[4,64,512]{2,1,0:T(8,128)} %gather_fusion.2), channel_id=1, source_target_pairs={{0,1},{1,2},{2,3},{3,4},{4,5},{5,6},{6,7},{7,0},{8,9},{9,10},{10,1... | collective-permute-start | bytes 1572872 | tf_op jit(solution)/shard_map/ppermute | solution.py:18
  26.8 82.2 %collective-permute-start.5 = (f32[4,64,512]{2,1,0:T(8,128)}, f32[4,64,512]{2,1,0:T(8,128)}, u32[]{:S(2)}, u32[]{:S(2)}) collective-permute-start(f32[4,64,512]{2,1,0:T(8,128)} %gather_fusion.3), channel_id=1, source_target_pairs={{0,7},{1,0},{2,1},{3,2},{4,3},{5,4},{6,5},{7,6},{8,15},{9,8},{10,9... | collective-permute-start | bytes 1572872 | tf_op jit(solution)/shard_map/ppermute | solution.py:18
  29.5 6.2 %copy-start.12 = (s32[5,32,4]{1,2,0:T(4,128)S(1)}, s32[5,32,4]{1,2,0:T(4,128)}, u32[]{:S(2)}) copy-start(s32[5,32,4]{1,2,0:T(4,128)} %param.11) | copy-start | bytes 7684
  29.5 6.6 %copy-start.13 = (s32[5,32]{1,0:T(8,128)S(1)}, s32[5,32]{1,0:T(8,128)}, u32[]{:S(2)}) copy-start(s32[5,32]{1,0:T(8,128)} %param.12) | copy-start | bytes 1924
  29.5 56.2 %collective-permute-start.1 = (f32[16,1,512]{2,1,0:T(1,128)S(1)}, f32[16,1,512]{2,1,0:T(1,128)S(1)}, u32[]{:S(2)}, u32[]{:S(2)}) collective-permute-start(f32[16,1,512]{2,1,0:T(1,128)S(1)} %slice.94), channel_id=1, source_target_pairs={{1,0},{2,1},{3,2},{4,3},{5,4},{6,5},{7,6},{9,8},{10,9},{11,10},{12... | collective-permute-start | bytes 98312 | tf_op jit(solution)/shard_map/ppermute | solution.py:12
  64.9 3.6 copy-start.11
  68.4 2.2 copy-start.4
  70.6 2.9 copy-start.5
  73.5 3.0 copy-start.1
  76.6 3.0 copy-start.2
  79.5 2.9 copy-start.3
  85.7 6.7 %collective-permute-start = (f32[1,32,512]{2,1,0:T(8,128)S(1)}, f32[1,32,512]{2,1,0:T(8,128)S(1)}, u32[]{:S(2)}, u32[]{:S(2)}) collective-permute-start(f32[1,32,512]{2,1,0:T(8,128)S(1)} %slice.91), channel_id=1, source_target_pairs={{8,0},{16,8},{24,16},{9,1},{17,9},{25,17},{10,2},{18,10},{26,18},{... | collective-permute-start | bytes 196616 | tf_op jit(solution)/shard_map/ppermute | solution.py:12
  101.0 2.4 copy-start.10
  136.4 14.0 %copy-start.9 = (f32[32,64,512]{2,1,0:T(8,128)S(1)}, f32[32,64,512]{2,1,0:T(8,128)}, u32[]{:S(2)}) copy-start(f32[32,64,512]{2,1,0:T(8,128)} %param.9) | copy-start | bytes 12582916
  196.5 26.5 %slice-start.4 = ((s8[16777216]{0:T(1024)(128)(4,1)}), s8[4194304]{0:T(1024)(128)(4,1)S(1)}, s32[]{:S(2)}) async-start(s8[16777216]{0:T(1024)(128)(4,1)} %bitcast.208), calls=%async_computation.5 | async-start | bytes 8388608
  196.5 26.5 %slice-start.5 = ((s8[16777216]{0:T(1024)(128)(4,1)}), s8[4194304]{0:T(1024)(128)(4,1)S(1)}, s32[]{:S(2)}) async-start(s8[16777216]{0:T(1024)(128)(4,1)} %bitcast.208), calls=%async_computation.6 | async-start | bytes 8388608
  196.5 26.5 %slice-start.6 = ((s8[16777216]{0:T(1024)(128)(4,1)}), s8[4194304]{0:T(1024)(128)(4,1)S(1)}, s32[]{:S(2)}) async-start(s8[16777216]{0:T(1024)(128)(4,1)} %bitcast.208), calls=%async_computation.7 | async-start | bytes 8388608
  212.6 10.4 %slice-start.7 = ((s8[16777216]{0:T(1024)(128)(4,1)}), s8[4194304]{0:T(1024)(128)(4,1)S(1)}, s32[]{:S(2)}) async-start(s8[16777216]{0:T(1024)(128)(4,1)} %bitcast.208), calls=%async_computation.8 | async-start | bytes 8388608
  212.6 10.4 %copy-start.6 = (f32[32,64,4,64]{3,2,1,0:T(4,128)S(1)}, f32[32,64,4,64]{3,2,1,0:T(4,128)}, u32[]{:S(2)}) copy-start(f32[32,64,4,64]{3,2,1,0:T(4,128)} %broadcast_multiply_fusion.2) | copy-start | bytes 6291460
  235.1 10.4 %copy-start.8 = (f32[32,64,4,64]{3,2,1,0:T(4,128)S(1)}, f32[32,64,4,64]{3,2,1,0:T(4,128)}, u32[]{:S(2)}) copy-start(f32[32,64,4,64]{3,2,1,0:T(4,128)} %broadcast_multiply_fusion.1) | copy-start | bytes 6291460
  245.5 25.3 %slice-start = ((s8[16777216]{0:T(1024)(128)(4,1)}), s8[4194304]{0:T(1024)(128)(4,1)S(1)}, s32[]{:S(2)}) async-start(s8[16777216]{0:T(1024)(128)(4,1)} %bitcast.203), calls=%async_computation.1 | async-start | bytes 8388608
  245.5 25.3 %slice-start.1 = ((s8[16777216]{0:T(1024)(128)(4,1)}), s8[4194304]{0:T(1024)(128)(4,1)S(1)}, s32[]{:S(2)}) async-start(s8[16777216]{0:T(1024)(128)(4,1)} %bitcast.203), calls=%async_computation.2 | async-start | bytes 8388608
  245.5 25.3 %slice-start.2 = ((s8[16777216]{0:T(1024)(128)(4,1)}), s8[4194304]{0:T(1024)(128)(4,1)S(1)}, s32[]{:S(2)}) async-start(s8[16777216]{0:T(1024)(128)(4,1)} %bitcast.203), calls=%async_computation.3 | async-start | bytes 8388608
  260.2 10.6 %slice-start.3 = ((s8[16777216]{0:T(1024)(128)(4,1)}), s8[4194304]{0:T(1024)(128)(4,1)S(1)}, s32[]{:S(2)}) async-start(s8[16777216]{0:T(1024)(128)(4,1)} %bitcast.203), calls=%async_computation.4 | async-start | bytes 8388608
  260.2 10.6 %copy-start.7 = (f32[32,64,4,64]{3,2,1,0:T(4,128)S(1)}, f32[32,64,4,64]{3,2,1,0:T(4,128)}, u32[]{:S(2)}) copy-start(f32[32,64,4,64]{3,2,1,0:T(4,128)} %broadcast_multiply_fusion) | copy-start | bytes 6291460
Sparse Core Ops, SparseCore 0:
  301.0 146.1 all-reduce.1
where the time goes:
time: 468 us; the launch traced here: 460 us
  waiting for transfers between devices  149 us (32%)
  local copies, waits for them, and re-layouts  132 us (28%)
  matrix products  131 us (28%)
  other arithmetic  23.7 us (5%)
  between operations  14.2 us (3%)
  starting transfers between devices  10.5 us (2%)
    psum x1, waiting for transfers between devices, body(): return lax.psum(partial_terms, ('gx', 'gy'))  146 us
    dot_general x5, matrix products, package_terms(): image = jnp.einsum('rinj,rnjk->rik', matrices, picked, precision=highest)  68.6 us
    gather x5, local copies, waits for them, and re-layouts, package_terms(): picked = table[columns[term_idx]]  63.7 us
    dot_general x5, matrix products, package_terms(): lax.dot_general(owned.reshape(-1, width), image.reshape(-1, width), (((0,...  49.6 us
    another operation x5, local copies, waits for them, and re-layouts, package_terms(): blocks[term_idx].reshape(row_count, block, entries, block)  23.8 us
    mul x5, other arithmetic, package_terms(): blocks[term_idx].reshape(row_count, block, entries, block)  14.7 us
    unnamed x48, local copies, waits for them, and re-layouts  13 us
    dot_general x6, matrix products, weighted_gram(): lax.dot_general(flat, scaled, (((0,), (0,)), ((), ())), precision=highest...  12.7 us
  transfers between devices with their start and end apart: 7, of which 2 were waited for; matrix products, arithmetic and copies ran while one was open for 18% of the time, Pallas kernels for 0%

commit v1 on v0

--- a/solution.py
+++ b/solution.py
@@ -87,7 +87,7 @@
     )
     partial_terms = die_terms(die_basis, die_coeff, next_x_row, next_y_col)
     partial_terms = partial_terms + package_terms(pkg_basis, table, columns, counts, pkg_blocks)
-    return lax.psum(partial_terms, ("gx", "gy"))
+    return lax.psum(lax.psum(partial_terms, "gy"), "gx")
 
 
 def solution(mesh):

time: 468 us -> 607 us (1.30)
  waiting for transfers between devices: 149 us -> 285 us
    psum x1 -> x2, waiting for transfers between devices: 146 us -> 282 us  [body(): return lax.psum(lax.psum(partial_terms, 'gy'), 'gx')]
    unnamed x48 -> x44, local copies, waits for them, and re-layouts: 13 us -> 13 us
  transfers between devices with their start and end apart: 7 -> 8, of which waited for: 2 -> 3; matrix products, arithmetic and copies ran while one was open for 18% -> 14% of each run, Pallas kernels for 0% -> 0%
where the time goes in v1:
time: 607 us; the launch traced here: 599 us
  waiting for transfers between devices  285 us (47%)
  matrix products  134 us (22%)
  local copies, waits for them, and re-layouts  132 us (22%)
  other arithmetic  23.8 us (4%)
  between operations  14.2 us (2%)
  starting transfers between devices  10.5 us (2%)
    psum x2, waiting for transfers between devices, body(): return lax.psum(lax.psum(partial_terms, 'gy'), 'gx')  282 us
    dot_general x5, matrix products, package_terms(): image = jnp.einsum('rinj,rnjk->rik', matrices, picked, precision=highest)  71.7 us
    gather x5, local copies, waits for them, and re-layouts, package_terms(): picked = table[columns[term_idx]]  63.7 us
    dot_general x5, matrix products, package_terms(): lax.dot_general(owned.reshape(-1, width), image.reshape(-1, width), (((0,...  49.6 us
    another operation x5, local copies, waits for them, and re-layouts, package_terms(): blocks[term_idx].reshape(row_count, block, entries, block)  23.8 us
    mul x5, other arithmetic, package_terms(): blocks[term_idx].reshape(row_count, block, entries, block)  14.7 us
    unnamed x44, local copies, waits for them, and re-layouts  13 us
    dot_general x6, matrix products, weighted_gram(): lax.dot_general(flat, scaled, (((0,), (0,)), ((), ())), precision=highest...  12.8 us
  transfers between devices with their start and end apart: 8, of which 3 were waited for; matrix products, arithmetic and copies ran while one was open for 14% of the time, Pallas kernels for 0%

profile of v1, /device:TPU:0, one launch (start us, length us, event | category | flops | bytes accessed | tf_op | source)
XLA Modules:
  0.0 599.2 jit_solution(4853784650961317529)
XLA Ops:
  7.4 3.6 gather_fusion
  11.0 3.1 collective-permute-start.2
  14.0 3.6 gather_fusion.1
  17.6 2.0 collective-permute-start.3
  19.6 3.6 gather_fusion.2
  23.2 3.6 gather_fusion.3
  26.8 2.6 collective-permute-start.5
  30.8 4.9 constant_dynamic-update-slice_fusion.4
  36.1 8.0 %fusion.120 = (f32[1,32,64,256]{3,2,1,0:T(8,128)S(1)}, f32[1,32,64,256]{3,2,1,0:T(8,128)}, f32[1,32,64,256]{3,2,1,0:T(8,128)}, f32[1,32,64,256]{3,2,1,0:T(8,128)}, f32[1,32,64,256]{3,2,1,0:T(8,128)}) fusion(f32[5,32,64,256]{3,2,1,0:T(8,128)} %param.13), kind=kLoop, calls=%fused_computation.128 | loop fusion | bytes 20971520 | tf_op jit(solution)/shard_map/slice | solution.py:62
  44.0 5.1 reshape_squeeze.22
  49.3 5.1 reshape_squeeze.10
  54.3 5.1 reshape_squeeze.23
  59.8 5.1 reshape_squeeze.24
  64.9 3.5 reshape_squeeze.25
  68.5 2.0 fusion.35
  70.6 2.9 broadcast_multiply_fusion.3
  73.6 3.0 broadcast_multiply_fusion.4
  76.6 2.9 broadcast_multiply_fusion.2
  79.6 2.9 broadcast_multiply_fusion.1
  82.5 3.0 broadcast_multiply_fusion
  87.2 2.2 fusion.59
  89.5 3.0 collective-permute-done
  92.5 2.2 fusion.41
  94.6 2.2 fusion.47
  96.9 2.0 fusion.53
  98.8 2.2 fusion.98
  101.0 2.3 copy-done.8
  105.3 1.9 constant_dynamic-update-slice_fusion.2
  107.2 1.9 constant_dynamic-update-slice_fusion.1
  110.9 12.9 %gather_fusion.5 = f32[128,64,512]{2,1,0:T(8,128)} fusion(f32[48,64,512]{2,1,0:T(8,128)} %constant_dynamic-update-slice_fusion, s32[1024]{0:T(1024)S(1)} %get-tuple-element.32), kind=kCustom, calls=%fused_computation.5 | custom fusion | bytes 33554944 | tf_op jit(solution)/shard_map/gather | solution.py:57
  123.8 12.7 %gather_fusion.4 = f32[128,64,512]{2,1,0:T(8,128)} fusion(f32[48,64,512]{2,1,0:T(8,128)} %constant_dynamic-update-slice_fusion, s32[1024]{0:T(1024)S(1)} %pad_clamp_fusion.4), kind=kCustom, calls=%fused_computation.4 | custom fusion | bytes 33554944 | tf_op jit(solution)/shard_map/gather | solution.py:57
  136.5 13.9 %fusion.18 = f32[32,64,512,1]{2,1,3,0:T(8,128)S(1)} fusion(f32[32,4,64,512]{3,2,1,0:T(8,128)} %bitcast.211, f32[32,64,4,64]{3,2,1,0:T(4,128)} %broadcast_multiply_fusion.4), kind=kOutput, calls=%fused_computation.27 | convolution fusion | flops 3221225472 | bytes 23068672 | tf_op jit(solution)/shard_map/rinj,rnjk->rik/dot_general | solution.py:64
  150.4 8.0 %fusion.65 = f32[5,512,512]{1,2,0:T(8,128)} fusion(f32[32,64,512]{2,1,0:T(8,128)S(1)} %copy-done.7, f32[32,64,512,1]{2,1,3,0:T(8,128)S(1)} %fusion.18), kind=kOutput, calls=%fused_computation.57 | convolution fusion | flops 6442450944 | bytes 9437184 | tf_op jit(solution)/shard_map/dot_general | solution.py:66
  158.4 12.7 %gather_fusion.6 = f32[128,64,512]{2,1,0:T(8,128)} fusion(f32[48,64,512]{2,1,0:T(8,128)} %constant_dynamic-update-slice_fusion, s32[1024]{0:T(1024)S(1)} %get-tuple-element.31), kind=kCustom, calls=%fused_computation.6 | custom fusion | bytes 33554944 | tf_op jit(solution)/shard_map/gather | solution.py:57
  171.1 12.7 %gather_fusion.7 = f32[128,64,512]{2,1,0:T(8,128)} fusion(f32[48,64,512]{2,1,0:T(8,128)} %constant_dynamic-update-slice_fusion, s32[1024]{0:T(1024)S(1)} %get-tuple-element.30), kind=kCustom, calls=%fused_computation.7 | custom fusion | bytes 33554944 | tf_op jit(solution)/shard_map/gather | solution.py:57
  183.8 12.9 %gather_fusion.8 = f32[128,64,512]{2,1,0:T(8,128)} fusion(f32[48,64,512]{2,1,0:T(8,128)} %constant_dynamic-update-slice_fusion, s32[1024]{0:T(1024)S(1)} %get-tuple-element.29), kind=kCustom, calls=%fused_computation.8 | custom fusion | bytes 33554944 | tf_op jit(solution)/shard_map/gather | solution.py:57
  196.6 16.0 %fusion.16 = f32[32,64,512,1]{2,1,3,0:T(8,128)} fusion(f32[32,4,64,512]{3,2,1,0:T(8,128)} %bitcast.206, f32[32,64,4,64]{3,2,1,0:T(4,128)} %broadcast_multiply_fusion.3), kind=kOutput, calls=%fused_computation.25 | convolution fusion | flops 3221225472 | bytes 23068672 | tf_op jit(solution)/shard_map/rinj,rnjk->rik/dot_general | solution.py:64
  212.7 10.4 %fusion.71 = f32[5,512,512]{1,2,0:T(8,128)} fusion(f32[5,512,512]{1,2,0:T(8,128)} %fusion.65, f32[32,64,512]{2,1,0:T(8,128)} %param.9, f32[32,64,512,1]{2,1,3,0:T(8,128)} %fusion.16), kind=kOutput, calls=%fused_computation.59 | convolution fusion | flops 6442450944 | bytes 9437184 | tf_op jit(solution)/shard_map/dot_general | solution.py:66
  223.1 13.6 %fusion.14 = f32[32,64,512,1]{2,1,3,0:T(8,128)} fusion(f32[32,4,64,512]{3,2,1,0:T(8,128)S(1)} %bitcast.210, f32[32,64,4,64]{3,2,1,0:T(4,128)} %broadcast_multiply_fusion.2), kind=kOutput, calls=%fused_computation.23 | convolution fusion | flops 3221225472 | bytes 23068672 | tf_op jit(solution)/shard_map/rinj,rnjk->rik/dot_general | solution.py:64
  236.7 10.4 %fusion.77 = f32[5,512,512]{1,2,0:T(8,128)} fusion(f32[5,512,512]{1,2,0:T(8,128)} %fusion.71, f32[32,64,512]{2,1,0:T(8,128)} %param.9, f32[32,64,512,1]{2,1,3,0:T(8,128)} %fusion.14), kind=kOutput, calls=%fused_computation.61 | convolution fusion | flops 6442450944 | bytes 9437184 | tf_op jit(solution)/shard_map/dot_general | solution.py:66
  247.1 14.7 %fusion.12 = f32[32,64,512,1]{2,1,3,0:T(8,128)} fusion(f32[32,4,64,512]{3,2,1,0:T(8,128)} %bitcast.207, f32[32,64,4,64]{3,2,1,0:T(4,128)S(1)} %copy-done.6), kind=kOutput, calls=%fused_computation.21 | convolution fusion | flops 3221225472 | bytes 23068672 | tf_op jit(solution)/shard_map/rinj,rnjk->rik/dot_general | solution.py:64
  261.8 10.6 %fusion.83 = f32[5,512,512]{1,2,0:T(8,128)} fusion(f32[5,512,512]{1,2,0:T(8,128)} %fusion.77, f32[32,64,512]{2,1,0:T(8,128)} %param.9, f32[32,64,512,1]{2,1,3,0:T(8,128)} %fusion.12), kind=kOutput, calls=%fused_computation.63 | convolution fusion | flops 6442450944 | bytes 9437184 | tf_op jit(solution)/shard_map/dot_general | solution.py:66
  272.4 13.4 %fusion.10 = f32[32,64,512,1]{2,1,3,0:T(8,128)} fusion(f32[32,4,64,512]{3,2,1,0:T(8,128)S(1)} %bitcast.205, f32[32,64,4,64]{3,2,1,0:T(4,128)} %broadcast_multiply_fusion), kind=kOutput, calls=%fused_computation.19 | convolution fusion | flops 3221225472 | bytes 23068672 | tf_op jit(solution)/shard_map/rinj,rnjk->rik/dot_general | solution.py:64
  285.8 10.2 %fusion.89 = f32[5,512,512]{1,2,0:T(8,128)} fusion(f32[5,512,512]{1,2,0:T(8,128)} %fusion.83, f32[32,64,512]{2,1,0:T(8,128)} %param.9, f32[32,64,512,1]{2,1,3,0:T(8,128)} %fusion.10), kind=kOutput, calls=%fused_computation.65 | convolution fusion | flops 6442450944 | bytes 9437184 | tf_op jit(solution)/shard_map/dot_general | solution.py:66
  296.1 7.9 %add.110 = f32[5,512,512]{1,2,0:T(8,128)} add(f32[5,512,512]{1,2,0:T(8,128)} %copy-done.8, f32[5,512,512]{1,2,0:T(8,128)} %fusion.89) | non-fusion elementwise | flops 1310720 | bytes 15728640 | tf_op jit(solution)/shard_map/add | solution.py:89
  304.1 90.6 %all-reduce.3.cloned.1.call-done = f32[5,512,512]{1,2,0:T(8,128)} async-done(((f32[5,512,512]{1,2,0:T(8,128)}), f32[5,512,512]{1,2,0:T(8,128)}) %all-reduce.3.cloned.1.call-update) | async-done | bytes 5242896 | tf_op jit(solution)/shard_map/psum | solution.py:90
  394.7 191.4 %all-reduce.5.cloned.1.call-done = f32[5,512,512]{1,2,0:T(8,128)} async-done(((f32[5,512,512]{1,2,0:T(8,128)}), f32[5,512,512]{1,2,0:T(8,128)}) %all-reduce.5.cloned.1.call-update) | async-done | bytes 5242896 | tf_op jit(solution)/shard_map/psum | solution.py:90
  586.1 5.9 copy.27
  (83 shorter events, 9.0 us)
Async XLA Ops:
  6.5 22.9 %copy-start = (f32[16,32,512]{2,1,0:T(8,128)S(1)}, f32[16,32,512]{2,1,0:T(8,128)}, u32[]{:S(2)}) copy-start(f32[16,32,512]{2,1,0:T(8,128)} %param.7) | copy-start | bytes 3145732
  6.5 388.1 %all-reduce.3.cloned.1.call-start = ((), (), s32[]{:S(2)}) async-start(), calls=%async_computation | async-start | bytes 10485760 | tf_op jit(solution)/shard_map/psum | solution.py:90
  11.0 92.4 %collective-permute-start.2 = (f32[4,64,512]{2,1,0:T(8,128)}, f32[4,64,512]{2,1,0:T(8,128)}, u32[]{:S(2)}, u32[]{:S(2)}) collective-permute-start(f32[4,64,512]{2,1,0:T(8,128)} %gather_fusion), channel_id=1, source_target_pairs={{0,8},{8,16},{16,24},{24,0},{1,9},{9,17},{17,25},{25,1},{2,10},{10... | collective-permute-start | bytes 1572872 | tf_op jit(solution)/shard_map/ppermute | solution.py:18
  17.6 87.7 %collective-permute-start.3 = (f32[4,64,512]{2,1,0:T(8,128)}, f32[4,64,512]{2,1,0:T(8,128)}, u32[]{:S(2)}, u32[]{:S(2)}) collective-permute-start(f32[4,64,512]{2,1,0:T(8,128)} %gather_fusion.1), channel_id=1, source_target_pairs={{0,24},{8,0},{16,8},{24,16},{1,25},{9,1},{17,9},{25,17},{2,26},{10... | collective-permute-start | bytes 1572872 | tf_op jit(solution)/shard_map/ppermute | solution.py:18
  23.2 83.9 %collective-permute-start.4 = (f32[4,64,512]{2,1,0:T(8,128)}, f32[4,64,512]{2,1,0:T(8,128)}, u32[]{:S(2)}, u32[]{:S(2)}) collective-permute-start(f32[4,64,512]{2,1,0:T(8,128)} %gather_fusion.2), channel_id=1, source_target_pairs={{0,1},{1,2},{2,3},{3,4},{4,5},{5,6},{6,7},{7,0},{8,9},{9,10},{10,1... | collective-permute-start | bytes 1572872 | tf_op jit(solution)/shard_map/ppermute | solution.py:18
  26.8 82.2 %collective-permute-start.5 = (f32[4,64,512]{2,1,0:T(8,128)}, f32[4,64,512]{2,1,0:T(8,128)}, u32[]{:S(2)}, u32[]{:S(2)}) collective-permute-start(f32[4,64,512]{2,1,0:T(8,128)} %gather_fusion.3), channel_id=1, source_target_pairs={{0,7},{1,0},{2,1},{3,2},{4,3},{5,4},{6,5},{7,6},{8,15},{9,8},{10,9... | collective-permute-start | bytes 1572872 | tf_op jit(solution)/shard_map/ppermute | solution.py:18
  29.4 6.2 %copy-start.10 = (s32[5,32,4]{1,2,0:T(4,128)S(1)}, s32[5,32,4]{1,2,0:T(4,128)}, u32[]{:S(2)}) copy-start(s32[5,32,4]{1,2,0:T(4,128)} %param.11) | copy-start | bytes 7684
  29.5 6.6 %copy-start.11 = (s32[5,32]{1,0:T(8,128)S(1)}, s32[5,32]{1,0:T(8,128)}, u32[]{:S(2)}) copy-start(s32[5,32]{1,0:T(8,128)} %param.12) | copy-start | bytes 1924
  29.5 56.3 %collective-permute-start.1 = (f32[16,1,512]{2,1,0:T(1,128)S(1)}, f32[16,1,512]{2,1,0:T(1,128)S(1)}, u32[]{:S(2)}, u32[]{:S(2)}) collective-permute-start(f32[16,1,512]{2,1,0:T(1,128)S(1)} %slice.94), channel_id=1, source_target_pairs={{1,0},{2,1},{3,2},{4,3},{5,4},{6,5},{7,6},{9,8},{10,9},{11,10},{12... | collective-permute-start | bytes 98312 | tf_op jit(solution)/shard_map/ppermute | solution.py:12
  64.9 3.6 copy-start.9
  68.4 2.2 copy-start.4
  70.6 2.9 copy-start.5
  73.6 3.0 copy-start.1
  76.6 3.0 copy-start.2
  79.6 2.9 copy-start.3
  85.8 6.7 %collective-permute-start = (f32[1,32,512]{2,1,0:T(8,128)S(1)}, f32[1,32,512]{2,1,0:T(8,128)S(1)}, u32[]{:S(2)}, u32[]{:S(2)}) collective-permute-start(f32[1,32,512]{2,1,0:T(8,128)S(1)} %slice.91), channel_id=1, source_target_pairs={{8,0},{16,8},{24,16},{9,1},{17,9},{25,17},{10,2},{18,10},{26,18},{... | collective-permute-start | bytes 196616 | tf_op jit(solution)/shard_map/ppermute | solution.py:12
  101.0 2.4 copy-start.8
  136.4 14.0 %copy-start.7 = (f32[32,64,512]{2,1,0:T(8,128)S(1)}, f32[32,64,512]{2,1,0:T(8,128)}, u32[]{:S(2)}) copy-start(f32[32,64,512]{2,1,0:T(8,128)} %param.9) | copy-start | bytes 12582916
  196.6 26.5 %slice-start.4 = ((s8[16777216]{0:T(1024)(128)(4,1)}), s8[4194304]{0:T(1024)(128)(4,1)S(1)}, s32[]{:S(2)}) async-start(s8[16777216]{0:T(1024)(128)(4,1)} %bitcast.208), calls=%async_computation.6 | async-start | bytes 8388608
  196.6 26.5 %slice-start.5 = ((s8[16777216]{0:T(1024)(128)(4,1)}), s8[4194304]{0:T(1024)(128)(4,1)S(1)}, s32[]{:S(2)}) async-start(s8[16777216]{0:T(1024)(128)(4,1)} %bitcast.208), calls=%async_computation.7 | async-start | bytes 8388608
  196.6 26.5 %slice-start.6 = ((s8[16777216]{0:T(1024)(128)(4,1)}), s8[4194304]{0:T(1024)(128)(4,1)S(1)}, s32[]{:S(2)}) async-start(s8[16777216]{0:T(1024)(128)(4,1)} %bitcast.208), calls=%async_computation.8 | async-start | bytes 8388608
  212.7 10.4 %slice-start.7 = ((s8[16777216]{0:T(1024)(128)(4,1)}), s8[4194304]{0:T(1024)(128)(4,1)S(1)}, s32[]{:S(2)}) async-start(s8[16777216]{0:T(1024)(128)(4,1)} %bitcast.208), calls=%async_computation.9 | async-start | bytes 8388608
  236.7 10.4 %copy-start.6 = (f32[32,64,4,64]{3,2,1,0:T(4,128)S(1)}, f32[32,64,4,64]{3,2,1,0:T(4,128)}, u32[]{:S(2)}) copy-start(f32[32,64,4,64]{3,2,1,0:T(4,128)} %broadcast_multiply_fusion.1) | copy-start | bytes 6291460
  247.1 25.3 %slice-start = ((s8[16777216]{0:T(1024)(128)(4,1)}), s8[4194304]{0:T(1024)(128)(4,1)S(1)}, s32[]{:S(2)}) async-start(s8[16777216]{0:T(1024)(128)(4,1)} %bitcast.203), calls=%async_computation.2 | async-start | bytes 8388608
  247.1 25.3 %slice-start.1 = ((s8[16777216]{0:T(1024)(128)(4,1)}), s8[4194304]{0:T(1024)(128)(4,1)S(1)}, s32[]{:S(2)}) async-start(s8[16777216]{0:T(1024)(128)(4,1)} %bitcast.203), calls=%async_computation.3 | async-start | bytes 8388608
  247.1 25.3 %slice-start.2 = ((s8[16777216]{0:T(1024)(128)(4,1)}), s8[4194304]{0:T(1024)(128)(4,1)S(1)}, s32[]{:S(2)}) async-start(s8[16777216]{0:T(1024)(128)(4,1)} %bitcast.203), calls=%async_computation.4 | async-start | bytes 8388608
  261.8 10.6 %slice-start.3 = ((s8[16777216]{0:T(1024)(128)(4,1)}), s8[4194304]{0:T(1024)(128)(4,1)S(1)}, s32[]{:S(2)}) async-start(s8[16777216]{0:T(1024)(128)(4,1)} %bitcast.203), calls=%async_computation.5 | async-start | bytes 8388608
  304.0 282.0 %all-reduce.5.cloned.1.call-start = ((), (), s32[]{:S(2)}) async-start(), calls=%async_computation.1 | async-start | bytes 10485760 | tf_op jit(solution)/shard_map/psum | solution.py:90
Sparse Core Ops, SparseCore 0:
  304.2 90.4 all-reduce.2
  397.0 188.9 all-reduce.4
